TPU v7x, 768 devices: a whole 4x8x12 slice. The times are simulated.
768 devices in a mesh: ctx: 64 (over x, y, core), head: 12 (over z).
Axes of the slice: x: 4, y: 8, z: 12, core: 2. Of those that a mesh axis runs over, the one named last changes fastest.
Arguments:
- query: bfloat16 [24576, 3072], P('ctx', 'head'), may hold values from -140 to 140
- key: bfloat16 [24576, 3072], P('ctx', 'head'), may hold values from -6 to 6
- value: bfloat16 [24576, 3072], P('ctx', 'head'), may hold values from -6 to 6
- block_mask: int32 [192, 3], P('ctx'), may hold values 0 or 1
- out_weight: bfloat16 [3072, 4096], P('head'), may hold values from -0.109375 to 0.109375
- cotangent: bfloat16 [24576, 4096], P(('ctx', 'head')), may hold values from -6 to 6
Outputs:
- mixed: bfloat16 [24576, 4096], P(('ctx', 'head'))
- grad_query: bfloat16 [24576, 3072], P('ctx', 'head')
- grad_key: bfloat16 [24576, 3072], P('ctx', 'head')
- grad_value: bfloat16 [24576, 3072], P('ctx', 'head')
All inputs are finite; a program needn't handle non-finite values. No bound on the sum of `block_mask` on one device may be relied on, other than what follows from the above.
Results may differ from a plain program's by a relative error of at most 0.006.
Values may be sent and summed in bfloat16 or wider, within the bound.
A program may use at most 64 MiB of HBM per device.

v0:
```python
import math

import jax
import jax.numpy as jnp
from jax import lax
from jax.sharding import PartitionSpec as P

DH = 128


def carried_in(part, axis, combine, identity, reverse):
    count = lax.axis_size(axis)
    place = lax.axis_index(axis)
    ahead = count - 1 - place if reverse else place
    gathered = lax.all_gather(part, axis)
    state = jnp.zeros_like(part) + jnp.asarray(identity, part.dtype)

    def one(lap, state):
        source = count - 1 - lap if reverse else lap
        return combine(state, lax.dynamic_index_in_dim(gathered, source, 0, False))

    return lax.fori_loop(0, ahead, one, state)


def keep_table(mask, rows):
    count = mask.shape[0]
    blk = rows // count
    full = jnp.broadcast_to((mask > 0)[:, None, :, None], (count, blk, count, blk)).reshape(
        rows, rows
    )
    pos = jnp.arange(rows)
    same = pos[:, None] // blk == pos[None, :] // blk
    causal = pos[:, None] >= pos[None, :]
    return (causal & (full | same), causal)


def add_one(earlier, later):
    return earlier + later


def on_device(query, key, value, block_mask, out_weight, cotangent):
    rows = query.shape[0]
    heads = query.shape[1] // DH
    width = heads * DH
    length = rows * lax.axis_size("ctx")
    scale = 1.0 / math.sqrt(DH * length)
    inv_root = 1.0 / math.sqrt(DH)
    single_float_type = jnp.float32
    upper_limit = lax.Precision.HIGHEST
    qh = query.reshape(rows, heads, DH).transpose(1, 0, 2)
    kh = key.reshape(rows, heads, DH).transpose(1, 0, 2)
    vh = value.reshape(rows, heads, DH).transpose(1, 0, 2)
    keep, causal = keep_table(block_mask, rows)
    grad_attn = jnp.einsum(
        "rn,kn->rk",
        lax.all_gather(cotangent, "head", axis=0, tiled=True),
        out_weight,
        preferred_element_type=single_float_type,
    ).astype(jnp.bfloat16)
    gradient_heads = grad_attn.reshape(rows, heads, DH).transpose(1, 0, 2)
    own_state = jnp.einsum("hjd,hje->hde", kh, vh, preferred_element_type=single_float_type)
    own_grad = scale * jnp.einsum(
        "hid,hie->hde", qh, gradient_heads, preferred_element_type=single_float_type
    )
    empty = jnp.zeros_like(own_state)
    linear_state = carried_in(own_state, "ctx", add_one, empty, False)
    grad_state = carried_in(own_grad, "ctx", add_one, empty, True)
    raw = jnp.einsum("hid,hjd->hij", qh, kh, preferred_element_type=single_float_type)
    scores = jnp.where(keep[None], raw * inv_root, -1e30)
    top = jnp.max(scores, -1, keepdims=True)
    expo = jnp.exp(scores - top)
    probs = (expo / jnp.sum(expo, -1, keepdims=True)).astype(jnp.bfloat16)
    soft = jnp.einsum("hij,hjd->hid", probs, vh, preferred_element_type=single_float_type)
    inner = jnp.where(causal[None], raw, 0.0).astype(jnp.bfloat16)
    intra = jnp.einsum("hij,hjd->hid", inner, vh, preferred_element_type=single_float_type)
    inter = jnp.einsum(
        "hid,hde->hie", qh.astype(single_float_type), linear_state, precision=upper_limit
    )
    attn_heads = (soft + scale * (intra + inter)).astype(jnp.bfloat16)
    attn = attn_heads.transpose(1, 0, 2).reshape(rows, width)
    partial_out = jnp.dot(attn, out_weight, preferred_element_type=single_float_type)
    mixed = lax.psum_scatter(partial_out, "head", scatter_dimension=0, tiled=True).astype(
        jnp.bfloat16
    )
    dprod = jnp.einsum("hid,hjd->hij", gradient_heads, vh, preferred_element_type=single_float_type)
    delta = jnp.sum(gradient_heads.astype(single_float_type) * soft, -1)
    dscore = (probs.astype(single_float_type) * (dprod - delta[:, :, None]) * inv_root).astype(
        jnp.bfloat16
    )
    dinner = jnp.where(causal[None], dprod, 0.0).astype(jnp.bfloat16)
    grad_q = jnp.einsum(
        "hij,hjd->hid", dscore, kh, preferred_element_type=single_float_type
    ) + scale * (
        jnp.einsum("hij,hjd->hid", dinner, kh, preferred_element_type=single_float_type)
        + jnp.einsum(
            "ykd,yod->yko",
            gradient_heads.astype(single_float_type),
            linear_state,
            precision=upper_limit,
        )
    )
    grad_k = (
        jnp.einsum("hij,hid->hjd", dscore, qh, preferred_element_type=single_float_type)
        + scale * jnp.einsum("hij,hid->hjd", dinner, qh, preferred_element_type=single_float_type)
        + jnp.einsum(
            "hjb,hab->hja", vh.astype(single_float_type), grad_state, precision=upper_limit
        )
    )
    value_gradient = (
        jnp.einsum("hij,hid->hjd", probs, gradient_heads, preferred_element_type=single_float_type)
        + scale
        * jnp.einsum(
            "hij,hid->hjd", inner, gradient_heads, preferred_element_type=single_float_type
        )
        + jnp.einsum(
            "hja,hab->hjb", kh.astype(single_float_type), grad_state, precision=upper_limit
        )
    )

    def flat(x):
        return x.astype(jnp.bfloat16).transpose(1, 0, 2).reshape(rows, width)

    return (mixed, flat(grad_q), flat(grad_k), flat(value_gradient))


def solution(mesh):
    return jax.shard_map(
        on_device,
        mesh=mesh,
        in_specs=(
            P("ctx", "head"),
            P("ctx", "head"),
            P("ctx", "head"),
            P("ctx", None),
            P("head", None),
            P(("ctx", "head"), None),
        ),
        out_specs=(P(("ctx", "head"), None), P("ctx", "head"), P("ctx", "head"), P("ctx", "head")),
        check_vma=False,
    )
```

profile of v0, /device:TPU:1, one launch (start us, length us, event | category | flops | bytes accessed | tf_op | source)
XLA Modules:
  0.0 367.6 jit_solution(15159412029201776238)
XLA Ops:
  8.0 1.9 fusion.24
  10.0 66.2 %all-gather.6.cloned.1.call-done = bf16[384,4096]{1,0:T(8,128)(2,1)} async-done(((bf16[32,4096]{1,0:T(8,128)(2,1)}), bf16[384,4096]{1,0:T(8,128)(2,1)}) %all-gather.6.cloned.1.call-update) | async-done | bytes 3145744 | tf_op jit(solution)/shard_map/all_gather | solution.py:56
  76.2 3.2 convolution_convert_fusion
  82.6 1.1 convolution_bitcast_fusion.3
  83.7 2.2 fusion.55
  85.9 1.4 divide_convert_fusion
  87.3 1.7 multiply_reduce_fusion
  88.9 89.3 %all-gather.8.cloned.1.call-done = f32[128,128,128]{2,1,0:T(8,128)} async-done(((f32[2,128,128]{2,1,0:T(8,128)}), f32[128,128,128]{2,1,0:T(8,128)}) %all-gather.8.cloned.1.call-update) | async-done | bytes 8388624 | tf_op jit(solution)/shard_map/all_gather | solution.py:15
  178.3 1.0 while.22
  179.2 1.5 fusion.14
  180.8 3.7 %fusion.56 = f32[384,4096]{1,0:T(8,128)} fusion(bf16[384,256]{0,1:T(8,128)(2,1)S(1)} %bitcast.228, bf16[256,4096]{1,0:T(8,128)(2,1)S(1)} %copy-done), kind=kOutput, calls=%fused_computation.83 | convolution fusion | flops 805306368 | bytes 8585216 | tf_op jit(solution)/shard_map/dot_general | solution.py:81
  184.5 1.1 multiply_convert_fusion
  187.0 1.1 fusion.13
  189.7 84.5 %all-gather.10.cloned.1.call-done = f32[128,128,128]{2,1,0:T(8,128)} async-done(((f32[2,128,128]{2,1,0:T(8,128)}), f32[128,128,128]{2,1,0:T(8,128)}) %all-gather.10.cloned.1.call-update) | async-done | bytes 8388624 | tf_op jit(solution)/shard_map/all_gather | solution.py:15
  274.1 59.6 %while.23 = (s32[]{:T(128)}, f32[2,128,128]{2,1,0:T(8,128)S(1)}, s32[]{:T(128)}, f32[64,2,128,128]{3,2,1,0:T(8,128)}, s32[]{:T(128)}, /*index=5*/s32[]{:T(128)}, s32[]{:T(128)}, s32[]{:T(128)}) while((s32[]{:T(128)}, f32[2,128,128]{2,1,0:T(8,128)S(1)}, s32[]{:T(128)}, f32[64,2,128,128]{3,2,1,0:T(8,128)}, s32[]{:T(128)}, /*index=5*/s32[]{:T(128)}, ...), condition=%wide.region_7.8_spmd, body=%wide.region_6.7_spmd.sunk | while | flops 32774 | bytes 393359 | solution.py:22
  290.5 0.9 bitcast_add_fusion.5
  291.4 1.0 bitcast_add_fusion.5
  298.2 0.9 bitcast_add_fusion.5
  300.1 0.9 bitcast_add_fusion.5
  301.1 0.9 bitcast_add_fusion.5
  303.0 0.9 bitcast_add_fusion.5
  303.9 0.9 bitcast_add_fusion.5
  305.9 0.9 bitcast_add_fusion.5
  309.7 0.9 bitcast_add_fusion.5
  312.6 0.9 bitcast_add_fusion.5
  313.6 0.9 bitcast_add_fusion.5
  324.2 0.9 bitcast_add_fusion.5
  328.0 0.9 bitcast_add_fusion.5
  330.9 0.9 bitcast_add_fusion.5
  333.8 1.4 fusion.16
  337.3 22.0 %reduce-scatter.2.cloned.1.call-done = f32[32,4096]{1,0:T(8,128)} async-done(((f32[384,4096]{1,0:T(8,128)}), f32[32,4096]{1,0:T(8,128)}) %reduce-scatter.2.cloned.1.call-update) | async-done | bytes 524304 | tf_op jit(solution)/shard_map/reduce_scatter | solution.py:82
  359.3 1.8 convert_element_type.50
  (97 shorter events, 54.9 us)
Async XLA Ops:
  7.2 69.0 %copy-start = (bf16[256,4096]{1,0:T(8,128)(2,1)S(1)}, bf16[256,4096]{1,0:T(8,128)(2,1)}, u32[]{:S(2)}) copy-start(bf16[256,4096]{1,0:T(8,128)(2,1)} %param.14) | copy-start | bytes 6291460
  7.2 69.0 %all-gather.6.cloned.1.call-start = ((), (), s32[]{:S(2)}) async-start(), calls=%async_computation.2 | async-start | bytes 3407872 | tf_op jit(solution)/shard_map/all_gather | solution.py:56
  7.9 170.3 %all-gather.8.cloned.1.call-start = ((), (), s32[]{:S(2)}) async-start(), calls=%async_computation.3 | async-start | bytes 8519680 | tf_op jit(solution)/shard_map/all_gather | solution.py:15
  9.9 69.4 %copy-start.2 = (bf16[384,256]{1,0:T(8,128)(2,1)S(1)}, bf16[384,256]{1,0:T(8,128)(2,1)}, u32[]{:S(2)}) copy-start(bf16[384,256]{1,0:T(8,128)(2,1)} %param.10) | copy-start | bytes 589828
  9.9 264.2 %all-gather.10.cloned.1.call-start = ((), (), s32[]{:S(2)}) async-start(), calls=%async_computation.4 | async-start | bytes 8519680 | tf_op jit(solution)/shard_map/all_gather | solution.py:15
  79.3 1.4 copy-start.8
  79.4 2.1 copy-start.3
  80.3 2.3 copy-start.1
  80.4 278.9 %reduce-scatter.2.cloned.1.call-start = ((), (), s32[]{:S(2)}) async-start(), calls=%async_computation.1 | async-start | bytes 6815744 | tf_op jit(solution)/shard_map/reduce_scatter | solution.py:82
  81.8 0.8 copy-start.6
  184.5 1.1 copy-start.4
  187.0 1.2 copy-start.7
  333.8 2.3 copy-start.5
Sparse Core Ops, SparseCore 0:
  10.4 65.7 all-gather.5
  80.7 97.5 all-gather.7
  182.8 91.2 all-gather.9
  277.1 82.1 reduce-scatter.1
where the time goes:
time: 369 us; the launch traced here: 368 us
  waiting for transfers between devices  263 us (71%)
  other arithmetic  62.5 us (17%)
  matrix products  21.9 us (6%)
  between operations  14 us (4%)
  local copies, waits for them, and re-layouts  4.87 us (1%)
    all_gather x2, waiting for transfers between devices, carried_in(): gathered = lax.all_gather(part, axis)  174 us
    all_gather x1, waiting for transfers between devices, on_device(): lax.all_gather(cotangent, 'head', axis=0, tiled=True)  66.2 us
    add x63, other arithmetic, add_one(): return earlier + later  59.1 us
    reduce_scatter x1, waiting for transfers between devices, on_device(): lax.psum_scatter(partial_out, 'head', scatter_dimension=0, tiled=True)  22 us
  transfers between devices with their start and end apart: 4, of which 4 were waited for; matrix products, arithmetic and copies ran while one was open for 24% of the time, Pallas kernels for 0%

commit v1 on v0

v1 whole, which is shorter than its diff:
```python
import functools
import math

import jax
import jax.numpy as jnp
from jax import lax
from jax.experimental import pallas as pl
from jax.experimental.pallas import tpu as pltpu
from jax.sharding import PartitionSpec as P

DH = 128
GROUP = 16
MESH = pl.DeviceIdType.MESH
F32 = jnp.float32
BF16 = jnp.bfloat16


def nn(a, b):
    return lax.dot_general(a, b, (((1,), (0,)), ((), ())), preferred_element_type=F32)


def nt(a, b):
    return lax.dot_general(a, b, (((1,), (1,)), ((), ())), preferred_element_type=F32)


def tn(a, b):
    return lax.dot_general(a, b, (((0,), (0,)), ((), ())), preferred_element_type=F32)


def two(x):
    high = x.astype(BF16)
    return high, (x - high.astype(F32)).astype(BF16)


class Scan:
    def __init__(self, sizes, reverse, part, heard, sums, total, others, result, sems):
        self.group, self.groups = sizes
        self.reverse = reverse
        self.part, self.heard, self.sums = part, heard, sums
        self.total, self.others, self.result = total, others, result
        self.send1, self.recv1, self.send2, self.recv2, self.send3, self.recv3 = sems
        ctx = lax.axis_index("ctx")
        self.r = lax.rem(ctx, self.group)
        self.x = lax.div(ctx, self.group)

    def peer(self, k):
        return lax.rem(self.r + k, self.group)

    def origin(self, k):
        return lax.rem(self.r + self.group - k, self.group)

    def copy1(self, k):
        j = self.peer(k)
        return pltpu.make_async_remote_copy(
            self.part.at[j], self.heard.at[self.r], self.send1.at[k], self.recv1.at[k],
            device_id={"ctx": self.x * self.group + j}, device_id_type=MESH,
        )

    def copy2(self, k):
        j = lax.rem(self.x + k, self.groups)
        return pltpu.make_async_remote_copy(
            self.total, self.others.at[self.x], self.send2.at[k], self.recv2.at[k],
            device_id={"ctx": j * self.group + self.r}, device_id_type=MESH,
        )

    def copy3(self, k):
        j = self.peer(k)
        return pltpu.make_async_remote_copy(
            self.sums.at[j], self.result.at[self.r], self.send3.at[k], self.recv3.at[k],
            device_id={"ctx": self.x * self.group + j}, device_id_type=MESH,
        )

    def each(self, first, last, what):
        def one(k, carry):
            what(k)
            return carry

        lax.fori_loop(first, last, one, 0)

    def start(self):
        self.each(1, self.group, lambda k: self.copy1(k).start())
        self.heard[self.r] = self.part[self.r]

    def middle(self):
        self.each(1, self.group, lambda k: self.copy1(k).wait_recv())
        order = range(self.group)
        acc = jnp.zeros(self.total.shape, F32)
        for p in reversed(order) if self.reverse else order:
            self.sums[p] = acc
            acc = acc + self.heard[p]
        self.total[...] = acc
        self.each(1, self.groups, lambda k: self.copy2(k).start())

    def back(self):
        self.each(1, self.groups, lambda k: self.copy2(k).wait_recv())
        base = jnp.zeros(self.total.shape, F32)
        for k in range(1, self.groups):
            j = lax.rem(self.x + self.groups - k, self.groups)
            before = j > self.x if self.reverse else j < self.x
            base = base + jnp.where(before, self.others[j], 0.0)
        for p in range(self.group):
            self.sums[p] = self.sums[p] + base
        self.each(1, self.group, lambda k: self.copy3(k).start())
        self.result[self.r] = self.sums[self.r]

    def finish(self):
        self.each(1, self.group, lambda k: self.copy3(k).wait_recv())

    def drain(self):
        self.each(1, self.group, lambda k: self.copy1(k).wait_send())
        self.each(1, self.groups, lambda k: self.copy2(k).wait_send())
        self.each(1, self.group, lambda k: self.copy3(k).wait_send())


def kernel(
    sizes, length,
    q_in, k_in, v_in, mask, w_in, cot_in,
    mixed_out, gq_out, gk_out, gv_out,
    q, k, v, w, cot, probs, inner, soft, intra, attn, part_out, g, dsc, din,
    gk_part, gv_part, gq, gk, gv, mixed, first, arrived,
    part, heard, sums, total, others, state,
    load_sem, store_sem, ag_send, ag_recv, rs_send, rs_recv, s1, r1, s2, r2, s3, r3,
):
    nz, group, groups = sizes
    rows = q_in.shape[0]
    blocks = mask.shape[0]
    blk = rows // blocks
    heads = q_in.shape[1] // DH
    scale = 1.0 / math.sqrt(DH * length)
    inv_root = 1.0 / math.sqrt(DH)
    z = lax.axis_index("head")
    ctx = lax.axis_index("ctx")
    up, down = lax.rem(z + 1, nz), lax.rem(z + nz - 1, nz)

    loads = [
        pltpu.make_async_copy(src, dst, load_sem.at[i])
        for i, (src, dst) in enumerate(
            ((k_in, k), (v_in, v), (q_in, q), (w_in, w), (cot_in, cot.at[z]))
        )
    ]
    for load in loads:
        load.start()

    barrier = pltpu.get_barrier_semaphore()
    r, x = lax.rem(ctx, group), lax.div(ctx, group)
    for neighbour in (up, down):
        pl.semaphore_signal(barrier, inc=1, device_id={"head": neighbour}, device_id_type=MESH)

    def greet(j, carry):
        peer = x * group + lax.rem(r + j, group)
        pl.semaphore_signal(barrier, inc=1, device_id={"ctx": peer}, device_id_type=MESH)
        return carry

    lax.fori_loop(1, group, greet, 0)

    def greet_far(j, carry):
        peer = lax.rem(x + j, groups) * group + r
        pl.semaphore_signal(barrier, inc=1, device_id={"ctx": peer}, device_id_type=MESH)
        return carry

    lax.fori_loop(1, groups, greet_far, 0)
    pl.semaphore_wait(barrier, 2 + group - 1 + groups - 1)

    streams = ((0, 0), (0, 1), (1, 0), (1, 1))
    hops = [nz // 2 if half == way else nz - 1 - nz // 2 for half, way in streams]

    def at(way, distance):
        step = distance if way == 0 else -distance
        return lax.rem(z + step + 2 * nz, nz)

    def ag_copy(t, s):
        half, way = streams[t]
        origin = at(way, -s)
        return pltpu.make_async_remote_copy(
            cot_in.at[half] if s == 0 else cot.at[origin, half],
            cot.at[origin, half],
            ag_send.at[t, s], ag_recv.at[t, s],
            device_id={"head": at(way, 1)}, device_id_type=MESH,
        )

    def ag_arrival(t, s):
        half, way = streams[t]
        here = cot.at[at(way, -s - 1), half]
        return pltpu.make_async_remote_copy(
            here, here, ag_send.at[t, s], ag_recv.at[t, s],
            device_id={"head": at(way, 1)}, device_id_type=MESH,
        )

    def ag_forward(s):
        for t in range(4):
            if s < hops[t]:
                if s > 0:
                    ag_arrival(t, s - 1).wait_recv()
                ag_copy(t, s).start()

    def rs_copy(t, s):
        return pltpu.make_async_remote_copy(
            first.at[t] if s == 0 else arrived.at[t, s - 1],
            arrived.at[t, s],
            rs_send.at[t, s], rs_recv.at[t, s],
            device_id={"head": at(streams[t][1], 1)}, device_id_type=MESH,
        )

    def rs_forward(s):
        for t in range(4):
            half, way = streams[t]
            if s < hops[t]:
                own = part_out[at(way, hops[t] - s), half]
                if s == 0:
                    first[t] = own.astype(BF16)
                else:
                    rs_copy(t, s - 1).wait_recv()
                    arrived[t, s - 1] = (arrived[t, s - 1].astype(F32) + own).astype(BF16)
                rs_copy(t, s).start()

    def scan(which):
        return Scan(
            (group, groups), which == 1,
            part.at[which], heard.at[which], sums.at[which], total.at[which],
            others.at[which], state.at[which],
            [sem.at[which] for sem in (s1, r1, s2, r2, s3, r3)],
        )

    linear, trailing = scan(0), scan(1)
    per_head = group // heads
    tri = lax.broadcasted_iota(jnp.int32, (blk, blk), 0) >= lax.broadcasted_iota(
        jnp.int32, (blk, blk), 1
    )

    def cols(h):
        return slice(h * DH, (h + 1) * DH)

    def put_part(which, h, value):
        part[which, h * per_head : (h + 1) * per_head] = value.reshape(per_head, -1, DH)

    def get_state(which, h):
        return state[which, h * per_head : (h + 1) * per_head].reshape(DH, DH)

    def causal(x, i, other):
        last = jnp.where(tri, x[:, i * blk :], other)
        return jnp.concatenate([x[:, : i * blk], last], 1) if i else last

    def softmax_part(h):
        for i in range(blocks):
            here, upto = slice(i * blk, (i + 1) * blk), slice(0, (i + 1) * blk)
            raw = nt(q[here, cols(h)], k[upto, cols(h)])
            scores = causal(raw * inv_root, i, -1e30)
            pieces = [
                jnp.where(mask[i, j] > 0, scores[:, j * blk : (j + 1) * blk], -1e30)
                for j in range(i)
            ]
            scores = jnp.concatenate(pieces + [scores[:, i * blk :]], 1)
            expo = jnp.exp(scores - jnp.max(scores, -1, keepdims=True))
            p = (expo / jnp.sum(expo, -1, keepdims=True)).astype(BF16)
            a = causal(raw, i, 0.0).astype(BF16)
            probs[h, here, upto] = p
            inner[h, here, upto] = a
            soft[h, here] = nn(p, v[upto, cols(h)])
            intra[h, here] = nn(a, v[upto, cols(h)])

    def attn_part(h):
        high, low = two(get_state(0, h))
        inter = nn(q[:, cols(h)], high) + nn(q[:, cols(h)], low)
        attn[:, cols(h)] = (soft[h] + scale * (intra[h] + inter)).astype(BF16)

    tile = min(512, w_in.shape[1])
    tiles = w_in.shape[1] // tile

    def project(lo, hi):
        def one(n, carry):
            c = pl.ds(pl.multiple_of(n * tile, tile), tile)
            part_out[:, :, :, c] = nn(attn[...], w[:, c]).reshape(nz, 2, -1, tile)
            return carry

        lax.fori_loop(lo, hi, one, 0)

    def grad_attn_part(i):
        n = nz // blocks
        g[i * blk : (i + 1) * blk] = nt(
            cot[i * n : (i + 1) * n].reshape(blk, w_in.shape[1]), w[...]
        ).astype(BF16)

    def backward_rows(h):
        high, low = two(get_state(0, h))
        for i in range(blocks):
            here, upto = slice(i * blk, (i + 1) * blk), slice(0, (i + 1) * blk)
            gi = g[here, cols(h)]
            dprod = nt(gi, v[upto, cols(h)])
            delta = jnp.sum(gi.astype(F32) * soft[h, here], -1, keepdims=True)
            ds = (probs[h, here, upto].astype(F32) * (dprod - delta) * inv_root).astype(BF16)
            di = causal(dprod, i, 0.0).astype(BF16)
            dsc[h, here, upto] = ds
            din[h, here, upto] = di
            kk = k[upto, cols(h)]
            gq[here, cols(h)] = (
                nn(ds, kk) + scale * (nn(di, kk) + (nt(gi, high) + nt(gi, low)))
            ).astype(BF16)

    def backward_columns(h):
        for j in range(blocks):
            here, below = slice(j * blk, (j + 1) * blk), slice(j * blk, rows)
            qq, gg = q[below, cols(h)], g[below, cols(h)]
            gk_part[here, cols(h)] = tn(dsc[h, below, here], qq) + scale * tn(
                din[h, below, here], qq
            )
            gv_part[here, cols(h)] = tn(probs[h, below, here], gg) + scale * tn(
                inner[h, below, here], gg
            )

    def backward_last(h):
        high, low = two(get_state(1, h))
        vv, kk = v[:, cols(h)], k[:, cols(h)]
        gk[:, cols(h)] = (gk_part[:, cols(h)] + (nt(vv, high) + nt(vv, low))).astype(BF16)
        gv[:, cols(h)] = (gv_part[:, cols(h)] + (nn(kk, high) + nn(kk, low))).astype(BF16)

    def store(i, src, dst):
        return pltpu.make_async_copy(src, dst, store_sem.at[i])

    ag_forward(0)
    loads[0].wait()
    loads[1].wait()
    for h in range(heads):
        put_part(0, h, tn(k[:, cols(h)], v[:, cols(h)]))
    linear.start()
    loads[2].wait()
    softmax_part(0)
    ag_forward(1)
    for h in range(1, heads):
        softmax_part(h)
    linear.middle()
    ag_forward(2)
    linear.back()
    ag_forward(3)
    linear.finish()
    for h in range(heads):
        attn_part(h)
    loads[3].wait()
    project(0, tiles // 2)
    ag_forward(4)
    project(tiles // 2, tiles)
    for s in range(5, max(hops)):
        ag_forward(s)

    rs_forward(0)
    loads[4].wait()
    for t in range(4):
        ag_arrival(t, hops[t] - 1).wait_recv()
    for i in range(blocks):
        grad_attn_part(i)
    rs_forward(1)
    for h in range(heads):
        put_part(1, h, scale * tn(q[:, cols(h)], g[:, cols(h)]))
    trailing.start()
    backward_rows(0)
    rs_forward(2)
    for h in range(1, heads):
        backward_rows(h)
    store(0, gq, gq_out).start()
    trailing.middle()
    rs_forward(3)
    backward_columns(0)
    trailing.back()
    rs_forward(4)
    for h in range(1, heads):
        backward_columns(h)
    trailing.finish()
    for h in range(heads):
        backward_last(h)
    store(1, gk, gk_out).start()
    store(2, gv, gv_out).start()
    for s in range(5, max(hops)):
        rs_forward(s)
    for half in range(2):
        acc = part_out[z, half]
        for t in range(4):
            if streams[t][0] == half:
                rs_copy(t, hops[t] - 1).wait_recv()
                acc = acc + arrived[t, hops[t] - 1].astype(F32)
        mixed[half] = acc.astype(BF16)
    store(3, mixed, mixed_out).start()

    for t in range(4):
        for s in range(hops[t]):
            ag_copy(t, s).wait_send()
            rs_copy(t, s).wait_send()
    linear.drain()
    trailing.drain()
    for i, (src, dst) in enumerate(((gq, gq_out), (gk, gk_out), (gv, gv_out), (mixed, mixed_out))):
        store(i, src, dst).wait()


def on_device(sizes, length, query, key, value, block_mask, out_weight, cotangent):
    nz, group, groups = sizes
    rows, width = query.shape
    heads = width // DH
    dim = out_weight.shape[1]
    sub = rows // nz // 2
    cotangent = cotangent.reshape(2, sub, dim)
    hop = nz // 2
    piece = (heads * DH // group, DH)
    vmem, dma = pltpu.VMEM, pltpu.SemaphoreType.DMA
    any_space = pl.BlockSpec(memory_space=pl.ANY)
    square = (heads, rows, rows)
    outs = pl.pallas_call(
        functools.partial(kernel, sizes, length),
        out_shape=(
            jax.ShapeDtypeStruct((2, sub, dim), BF16),
            jax.ShapeDtypeStruct((rows, width), BF16),
            jax.ShapeDtypeStruct((rows, width), BF16),
            jax.ShapeDtypeStruct((rows, width), BF16),
        ),
        in_specs=[any_space, any_space, any_space, pl.BlockSpec(memory_space=pltpu.SMEM), any_space, any_space],
        out_specs=(any_space,) * 4,
        scratch_shapes=[
            vmem((rows, width), BF16),
            vmem((rows, width), BF16),
            vmem((rows, width), BF16),
            vmem((width, dim), BF16),
            vmem((nz, 2, sub, dim), BF16),
            vmem(square, BF16),
            vmem(square, BF16),
            vmem((heads, rows, DH), F32),
            vmem((heads, rows, DH), F32),
            vmem((rows, width), BF16),
            vmem((nz, 2, sub, dim), F32),
            vmem((rows, width), BF16),
            vmem(square, BF16),
            vmem(square, BF16),
            vmem((rows, width), F32),
            vmem((rows, width), F32),
            vmem((rows, width), BF16),
            vmem((rows, width), BF16),
            vmem((rows, width), BF16),
            vmem((2, sub, dim), BF16),
            vmem((4, sub, dim), BF16),
            vmem((4, hop, sub, dim), BF16),
            vmem((2, group) + piece, F32),
            vmem((2, group) + piece, F32),
            vmem((2, group) + piece, F32),
            vmem((2,) + piece, F32),
            vmem((2, groups) + piece, F32),
            vmem((2, group) + piece, F32),
            dma((5,)),
            dma((4,)),
            dma((4, hop)),
            dma((4, hop)),
            dma((4, hop)),
            dma((4, hop)),
            dma((2, group)),
            dma((2, group)),
            dma((2, groups)),
            dma((2, groups)),
            dma((2, group)),
            dma((2, group)),
        ],
        compiler_params=pltpu.CompilerParams(
            collective_id=0, has_side_effects=True, vmem_limit_bytes=56 << 20
        ),
        name="mixer",
    )(query, key, value, block_mask, out_weight, cotangent)
    return (outs[0].reshape(2 * sub, dim),) + tuple(outs[1:])


def solution(mesh):
    ctx = mesh.shape["ctx"]
    sizes = (mesh.shape["head"], GROUP, ctx // GROUP)

    def step(query, key, value, block_mask, out_weight, cotangent):
        return on_device(
            sizes, query.shape[0] * ctx, query, key, value, block_mask, out_weight, cotangent
        )

    return jax.shard_map(
        step,
        mesh=mesh,
        in_specs=(
            P("ctx", "head"),
            P("ctx", "head"),
            P("ctx", "head"),
            P("ctx", None),
            P("head", None),
            P(("ctx", "head"), None),
        ),
        out_specs=(P(("ctx", "head"), None), P("ctx", "head"), P("ctx", "head"), P("ctx", "head")),
        check_vma=False,
    )
```

time: 369 us -> 95.2 us (0.26)
  waiting for transfers between devices: 263 us -> 0 us
  Pallas kernels: 0 us -> 87.7 us
  other arithmetic: 62.5 us -> 0 us
  matrix products: 21.9 us -> 0 us
  between operations: 14 us -> 0.64 us
    all_gather x3 -> x0, waiting for transfers between devices: 240 us -> none  [the longest x2 174 us: carried_in(): gathered = lax.all_gather(part, axis)]
    pallas_call x0 -> x1, Pallas kernels: none -> 87.7 us  [on_device(): pl.pallas_call(functools.partial(kernel, sizes, length), out_shape=(jax.S...]
    add x63 -> x0, other arithmetic: 59.1 us -> none  [add_one(): return earlier + later]
    reduce_scatter x1 -> x0, waiting for transfers between devices: 22 us -> none  [on_device(): lax.psum_scatter(partial_out, 'head', scatter_dimension=0, tiled=True)]
    dot_general x18 -> x0, matrix products: 19.7 us -> none  [the longest x1 3.71 us: on_device(): jnp.dot(attn, out_weight, preferred_element_type=single_float_type)]
  transfers between devices with their start and end apart: 4 -> 0, of which waited for: 4 -> 0; matrix products, arithmetic and copies ran while one was open for 24% -> 0% of each run, Pallas kernels for 0% -> 0%
where the time goes in v1:
time: 95.2 us; the launch traced here: 94.9 us
  Pallas kernels  87.7 us (92%)
  local copies, waits for them, and re-layouts  6.52 us (7%)
    pallas_call x1, Pallas kernels, on_device(): pl.pallas_call(functools.partial(kernel, sizes, length), out_shape=(jax.S...  87.7 us
    unnamed x4, local copies, waits for them, and re-layouts  6.52 us

profile of v1, /device:TPU:1, one launch (start us, length us, event | category | flops | bytes accessed | tf_op | source)
XLA Modules:
  0.0 94.9 jit_solution(12239224978465331182)
XLA Ops:
  0.6 87.7 %mixer.1 = (bf16[2,16,4096]{2,1,0:T(8,128)(2,1)}, bf16[384,256]{1,0:T(8,128)(2,1)}, bf16[384,256]{1,0:T(8,128)(2,1)}, bf16[384,256]{1,0:T(8,128)(2,1)}) custom-call(bf16[384,256]{1,0:T(8,128)(2,1)} %q_in.1, bf16[384,256]{1,0:T(8,128)(2,1)} %k_in.1, bf16[384,256]{1,0:T(8,128)(2,1)} %v_in.1, s32[3,3]{1,0:T(4,128)} %mask.1, bf16[256,4096]{1,0:T(8,128)(2,1)} %w_in.1, ...), custom_call_target="tpu_custom_call" | custom-call | tf_op jit(solution)/shard_map/mixer/pallas_call | solution.py:404
  88.4 1.7 %copy.14 = bf16[32,4096]{1,0:T(8,128)(2,1)} copy(bf16[32,4096]{1,0:T(8,128)(2,1)} %bitcast.3) | data formatting | bytes 524288
  90.0 1.6 %copy.15 = bf16[384,256]{1,0:T(8,128)(2,1)} copy(bf16[384,256]{1,0:T(8,128)(2,1)} %get-tuple-element.17) | data formatting | bytes 393216
  91.7 1.6 %copy.16 = bf16[384,256]{1,0:T(8,128)(2,1)} copy(bf16[384,256]{1,0:T(8,128)(2,1)} %get-tuple-element.18) | data formatting | bytes 393216
  93.3 1.6 %copy.17 = bf16[384,256]{1,0:T(8,128)(2,1)} copy(bf16[384,256]{1,0:T(8,128)(2,1)} %get-tuple-element.19) | data formatting | bytes 393216

commit v2 on v1

--- a/solution.py
+++ b/solution.py
@@ -10,6 +10,7 @@
 
 DH = 128
 GROUP = 16
+SHARE = 2
 MESH = pl.DeviceIdType.MESH
 F32 = jnp.float32
 BF16 = jnp.bfloat16
@@ -116,35 +117,50 @@
     sizes, length,
     q_in, k_in, v_in, mask, w_in, cot_in,
     mixed_out, gq_out, gk_out, gv_out,
-    q, k, v, w, cot, probs, inner, soft, intra, attn, part_out, g, dsc, din,
+    q, k, v, w, cot, probs, inner, soft, intra, attn, attn_sent, attn_held, part_out,
+    g_sent, g_heard, g_rows, g, dsc, din,
     gk_part, gv_part, gq, gk, gv, mixed, first, arrived,
     part, heard, sums, total, others, state,
     load_sem, store_sem, ag_send, ag_recv, rs_send, rs_recv, s1, r1, s2, r2, s3, r3,
+    wz_send, wz_recv, wx_send, wx_recv, wy_send, wy_recv, wc_send, wc_recv,
+    vy_send, vy_recv, vx_send, vx_recv, vc_send, vc_recv,
+    at_send, at_recv, gt_send, gt_recv,
 ):
-    nz, group, groups = sizes
-    rows = q_in.shape[0]
+    nz, group, groups, share = sizes
+    span = nz // share
+    lines = group // 2
+    rows, width = q_in.shape
+    dim = w_in.shape[-1]
     blocks = mask.shape[0]
     blk = rows // blocks
-    heads = q_in.shape[1] // DH
+    heads = width // DH
     scale = 1.0 / math.sqrt(DH * length)
     inv_root = 1.0 / math.sqrt(DH)
     z = lax.axis_index("head")
     ctx = lax.axis_index("ctx")
-    up, down = lax.rem(z + 1, nz), lax.rem(z + nz - 1, nz)
+    r, x = lax.rem(ctx, group), lax.div(ctx, group)
+    y, core = lax.div(r, 2), lax.rem(r, 2)
+
+    def along(distance):
+        return lax.rem(z + distance + 2 * nz, nz)
+
+    ahead = (span // 2, span - 1 - span // 2)
 
     loads = [
         pltpu.make_async_copy(src, dst, load_sem.at[i])
         for i, (src, dst) in enumerate(
-            ((k_in, k), (v_in, v), (q_in, q), (w_in, w), (cot_in, cot.at[z]))
+            ((k_in, k), (v_in, v), (q_in, q), (w_in, w.at[0]))
+            + tuple((cot_in.at[half], cot.at[half, ahead[half]]) for half in range(2))
         )
     ]
     for load in loads:
         load.start()
 
     barrier = pltpu.get_barrier_semaphore()
-    r, x = lax.rem(ctx, group), lax.div(ctx, group)
-    for neighbour in (up, down):
-        pl.semaphore_signal(barrier, inc=1, device_id={"head": neighbour}, device_id_type=MESH)
+    for distance in [1, -1] + [n * span for n in range(1, share)]:
+        pl.semaphore_signal(
+            barrier, inc=1, device_id={"head": along(distance)}, device_id_type=MESH
+        )
 
     def greet(j, carry):
         peer = x * group + lax.rem(r + j, group)
@@ -159,38 +175,31 @@
         return carry
 
     lax.fori_loop(1, groups, greet_far, 0)
-    pl.semaphore_wait(barrier, 2 + group - 1 + groups - 1)
+    pl.semaphore_wait(barrier, 2 + share - 1 + group - 1 + groups - 1)
 
     streams = ((0, 0), (0, 1), (1, 0), (1, 1))
-    hops = [nz // 2 if half == way else nz - 1 - nz // 2 for half, way in streams]
-
-    def at(way, distance):
-        step = distance if way == 0 else -distance
-        return lax.rem(z + step + 2 * nz, nz)
+    sign = (1, -1)
+    ag_hops = [ahead[half ^ way] for half, way in streams]
+    rs_hops = [ahead[1 ^ half ^ way] for half, way in streams]
+
+    def ag_slot(t, s):
+        half, way = streams[t]
+        return cot.at[half, ahead[half] - sign[way] * s]
 
     def ag_copy(t, s):
         half, way = streams[t]
-        origin = at(way, -s)
-        return pltpu.make_async_remote_copy(
-            cot_in.at[half] if s == 0 else cot.at[origin, half],
-            cot.at[origin, half],
+        return pltpu.make_async_remote_copy(
+            cot_in.at[half] if s == 0 else ag_slot(t, s),
+            ag_slot(t, s + 1),
             ag_send.at[t, s], ag_recv.at[t, s],
-            device_id={"head": at(way, 1)}, device_id_type=MESH,
-        )
-
-    def ag_arrival(t, s):
-        half, way = streams[t]
-        here = cot.at[at(way, -s - 1), half]
-        return pltpu.make_async_remote_copy(
-            here, here, ag_send.at[t, s], ag_recv.at[t, s],
-            device_id={"head": at(way, 1)}, device_id_type=MESH,
+            device_id={"head": along(sign[way])}, device_id_type=MESH,
         )
 
     def ag_forward(s):
         for t in range(4):
-            if s < hops[t]:
-                if s > 0:
-                    ag_arrival(t, s - 1).wait_recv()
+            if 0 < s <= ag_hops[t]:
+                ag_copy(t, s - 1).wait_recv()
+            if s < ag_hops[t]:
                 ag_copy(t, s).start()
 
     def rs_copy(t, s):
@@ -198,20 +207,205 @@
             first.at[t] if s == 0 else arrived.at[t, s - 1],
             arrived.at[t, s],
             rs_send.at[t, s], rs_recv.at[t, s],
-            device_id={"head": at(streams[t][1], 1)}, device_id_type=MESH,
+            device_id={"head": along(sign[streams[t][1]])}, device_id_type=MESH,
         )
 
     def rs_forward(s):
         for t in range(4):
             half, way = streams[t]
-            if s < hops[t]:
-                own = part_out[at(way, hops[t] - s), half]
+            if s < rs_hops[t]:
+                own = part_out[half, ahead[half] + sign[way] * (rs_hops[t] - s)]
                 if s == 0:
                     first[t] = own.astype(BF16)
                 else:
                     rs_copy(t, s - 1).wait_recv()
                     arrived[t, s - 1] = (arrived[t, s - 1].astype(F32) + own).astype(BF16)
                 rs_copy(t, s).start()
+
+    shared = pl.ds(1, share - 1)
+    wide = dim // 2
+    few = lines // groups
+    left = pl.ds(pl.multiple_of(x * (wide // groups), wide // groups), wide // groups)
+    right = pl.ds(pl.multiple_of(wide + y * (wide // lines), wide // lines), wide // lines)
+
+    def wz_copy(n, side):
+        if side:
+            at = (core, pl.ds(x * few, few), slice(None), right)
+        else:
+            at = (core, y, slice(None), left)
+        return pltpu.make_async_remote_copy(
+            w_in.at[at], w.at[(share - n,) + at], wz_send.at[side, n], wz_recv.at[side, n],
+            device_id={"head": along(n * span)}, device_id_type=MESH,
+        )
+
+    def wx_copy(n):
+        piece = w.at[shared, core, y, :, left]
+        return pltpu.make_async_remote_copy(
+            piece, piece, wx_send.at[n], wx_recv.at[n],
+            device_id={"ctx": lax.rem(x + n, groups) * group + r}, device_id_type=MESH,
+        )
+
+    wy_hops = [lines // 2 if half == way else lines - 1 - lines // 2 for half, way in streams]
+
+    def wy_piece(t, s):
+        half, way = streams[t]
+        from_y = lax.rem(y - sign[way] * s + lines, lines)
+        return w.at[shared, core, from_y, :, pl.ds(half * (wide // 2), wide // 2)]
+
+    def wy_copy(t, s):
+        to = lax.rem(y + sign[streams[t][1]] + lines, lines)
+        return pltpu.make_async_remote_copy(
+            wy_piece(t, s), wy_piece(t, s), wy_send.at[t, s], wy_recv.at[t, s],
+            device_id={"ctx": x * group + to * 2 + core}, device_id_type=MESH,
+        )
+
+    def to_core(piece, send, recv):
+        return pltpu.make_async_remote_copy(
+            piece, piece, send, recv,
+            device_id={"ctx": x * group + y * 2 + 1 - core}, device_id_type=MESH,
+        )
+
+    def wc_copy(t, s):
+        return to_core(wy_piece(t, s), wc_send.at[t, s], wc_recv.at[t, s])
+
+    def vy_copy(n):
+        piece = w.at[shared, core, pl.ds(x * few, few), :, right]
+        return pltpu.make_async_remote_copy(
+            piece, piece, vy_send.at[n], vy_recv.at[n],
+            device_id={"ctx": x * group + lax.rem(y + n, lines) * 2 + core}, device_id_type=MESH,
+        )
+
+    def vx_piece(way, s):
+        from_x = lax.rem(x - sign[way] * s + groups, groups)
+        halved = 2 * s == groups
+        columns = pl.ds(wide + way * (wide // 2), wide // 2) if halved else pl.ds(wide, wide)
+        return w.at[shared, core, pl.ds(from_x * few, few), :, columns]
+
+    vx_hops = groups // 2
+
+    def vx_copy(way, s):
+        from_x = lax.rem(x - sign[way] * s + groups, groups)
+        halved = 2 * (s + 1) == groups
+        columns = pl.ds(wide + way * (wide // 2), wide // 2) if halved else pl.ds(wide, wide)
+        piece = w.at[shared, core, pl.ds(from_x * few, few), :, columns]
+        to = lax.rem(x + sign[way] + groups, groups)
+        return pltpu.make_async_remote_copy(
+            piece, piece, vx_send.at[way, s], vx_recv.at[way, s],
+            device_id={"ctx": to * group + r}, device_id_type=MESH,
+        )
+
+    def vc_copy(way, s):
+        return to_core(vx_piece(way, s), vc_send.at[way, s], vc_recv.at[way, s])
+
+    wc_all = [(0, 0), (2, 0)] + [(t, s + 1) for t in range(4) for s in range(wy_hops[t])]
+    vc_all = [(0, 0)] + [(way, s + 1) for way in range(2) for s in range(vx_hops)]
+
+    def w_start():
+        for n in range(1, share):
+            for side in range(2):
+                wz_copy(n, side).start()
+
+    def w_spread():
+        for n in range(1, share):
+            wz_copy(n, 0).wait_recv()
+        for n in range(1, groups):
+            wx_copy(n).start()
+        for n in range(1, share):
+            wz_copy(n, 1).wait_recv()
+        for n in range(1, lines):
+            vy_copy(n).start()
+
+    def w_forward(s):
+        if s == 0:
+            for n in range(1, groups):
+                wx_copy(n).wait_recv()
+        for t in range(4):
+            if 0 < s <= wy_hops[t]:
+                wy_copy(t, s - 1).wait_recv()
+            if s < wy_hops[t]:
+                wy_copy(t, s).start()
+            if (t, s) in wc_all:
+                wc_copy(t, s).start()
+
+    def v_forward(s):
+        if s == 0:
+            for n in range(1, lines):
+                vy_copy(n).wait_recv()
+        for way in range(2):
+            if 0 < s <= vx_hops:
+                vx_copy(way, s - 1).wait_recv()
+            if s < vx_hops:
+                vx_copy(way, s).start()
+            if (way, s) in vc_all:
+                vc_copy(way, s).start()
+
+    def w_finish():
+        for t, s in wc_all:
+            wc_copy(t, s).wait_recv()
+        for way, s in vc_all:
+            vc_copy(way, s).wait_recv()
+
+    def w_drain():
+        for n in range(1, share):
+            for side in range(2):
+                wz_copy(n, side).wait_send()
+        for n in range(1, groups):
+            wx_copy(n).wait_send()
+        for t in range(4):
+            for s in range(wy_hops[t]):
+                wy_copy(t, s).wait_send()
+        for t, s in wc_all:
+            wc_copy(t, s).wait_send()
+        for n in range(1, lines):
+            vy_copy(n).wait_send()
+        for way in range(2):
+            for s in range(vx_hops):
+                vx_copy(way, s).wait_send()
+        for way, s in vc_all:
+            vc_copy(way, s).wait_send()
+
+    def token(n, half, i):
+        return along(n * span - ahead[half] + i)
+
+    def attn_copy(n):
+        return pltpu.make_async_remote_copy(
+            attn_sent.at[n], attn_held.at[share - n], at_send.at[n], at_recv.at[n],
+            device_id={"head": along(n * span)}, device_id_type=MESH,
+        )
+
+    def attn_exchange():
+        for n in range(1, share):
+            for half in range(2):
+                for i in range(span):
+                    attn_sent[n, half, i] = attn[token(n, half, i), half]
+            attn_copy(n).start()
+        for half in range(2):
+            for i in range(span):
+                attn_held[0, half, i] = attn[token(0, half, i), half]
+
+    def g_copy(n):
+        return pltpu.make_async_remote_copy(
+            g_sent.at[n], g_heard.at[share - n], gt_send.at[n], gt_recv.at[n],
+            device_id={"head": along(n * span)}, device_id_type=MESH,
+        )
+
+    def grad_attn_part(n):
+        value = nt(cot[...].reshape(-1, dim), w[n].reshape(width, dim)).astype(BF16)
+        value = value.reshape(2, span, -1, width)
+        if n == 0:
+            g_heard[0] = value
+        else:
+            g_sent[n] = value
+            g_copy(n).start()
+
+    def g_collect():
+        for n in range(1, share):
+            g_copy(n).wait_recv()
+        for n in range(share):
+            for half in range(2):
+                for i in range(span):
+                    g_rows[token(n, half, i), half] = g_heard[n, half, i]
+        g[...] = g_rows[...].reshape(rows, width)
 
     def scan(which):
         return Scan(
@@ -261,24 +455,24 @@
     def attn_part(h):
         high, low = two(get_state(0, h))
         inter = nn(q[:, cols(h)], high) + nn(q[:, cols(h)], low)
-        attn[:, cols(h)] = (soft[h] + scale * (intra[h] + inter)).astype(BF16)
-
-    tile = min(512, w_in.shape[1])
-    tiles = w_in.shape[1] // tile
-
-    def project(lo, hi):
+        value = (soft[h] + scale * (intra[h] + inter)).astype(BF16)
+        attn[:, :, :, cols(h)] = value.reshape(nz, 2, -1, DH)
+
+    tile = min(512, dim)
+    tiles = dim // tile
+
+    def project():
         def one(n, carry):
             c = pl.ds(pl.multiple_of(n * tile, tile), tile)
-            part_out[:, :, :, c] = nn(attn[...], w[:, c]).reshape(nz, 2, -1, tile)
+            acc = 0.0
+            for n in range(share):
+                acc = acc + nn(
+                    attn_held[n].reshape(-1, width), w[n, :, :, :, c].reshape(width, tile)
+                )
+            part_out[:, :, :, c] = acc.reshape(2, span, -1, tile)
             return carry
 
-        lax.fori_loop(lo, hi, one, 0)
-
-    def grad_attn_part(i):
-        n = nz // blocks
-        g[i * blk : (i + 1) * blk] = nt(
-            cot[i * n : (i + 1) * n].reshape(blk, w_in.shape[1]), w[...]
-        ).astype(BF16)
+        lax.fori_loop(0, tiles, one, 0)
 
     def backward_rows(h):
         high, low = two(get_state(0, h))
@@ -316,6 +510,7 @@
     def store(i, src, dst):
         return pltpu.make_async_copy(src, dst, store_sem.at[i])
 
+    w_start()
     ag_forward(0)
     loads[0].wait()
     loads[1].wait()
@@ -323,44 +518,54 @@
         put_part(0, h, tn(k[:, cols(h)], v[:, cols(h)]))
     linear.start()
     loads[2].wait()
+    w_spread()
     softmax_part(0)
     ag_forward(1)
+    linear.middle()
+    w_forward(0)
+    v_forward(0)
     for h in range(1, heads):
         softmax_part(h)
-    linear.middle()
+    w_forward(1)
+    linear.back()
     ag_forward(2)
-    linear.back()
+    w_forward(2)
+    v_forward(1)
+    w_forward(3)
     ag_forward(3)
     linear.finish()
     for h in range(heads):
         attn_part(h)
-    loads[3].wait()
-    project(0, tiles // 2)
-    ag_forward(4)
-    project(tiles // 2, tiles)
-    for s in range(5, max(hops)):
+    attn_exchange()
+    v_forward(2)
+    for s in range(4, max(wy_hops) + 1):
+        w_forward(s)
+    for s in range(4, max(ag_hops) + 1):
         ag_forward(s)
-
+    w_finish()
+
+    for load in loads[3:]:
+        load.wait()
+    for n in reversed(range(share)):
+        grad_attn_part(n)
+    for n in range(1, share):
+        attn_copy(n).wait_recv()
+    project()
     rs_forward(0)
-    loads[4].wait()
-    for t in range(4):
-        ag_arrival(t, hops[t] - 1).wait_recv()
-    for i in range(blocks):
-        grad_attn_part(i)
-    rs_forward(1)
+    g_collect()
     for h in range(heads):
         put_part(1, h, scale * tn(q[:, cols(h)], g[:, cols(h)]))
     trailing.start()
     backward_rows(0)
-    rs_forward(2)
+    rs_forward(1)
     for h in range(1, heads):
         backward_rows(h)
     store(0, gq, gq_out).start()
     trailing.middle()
-    rs_forward(3)
+    rs_forward(2)
     backward_columns(0)
     trailing.back()
-    rs_forward(4)
+    rs_forward(3)
     for h in range(1, heads):
         backward_columns(h)
     trailing.finish()
@@ -368,61 +573,86 @@
         backward_last(h)
     store(1, gk, gk_out).start()
     store(2, gv, gv_out).start()
-    for s in range(5, max(hops)):
+    for s in range(4, max(rs_hops)):
         rs_forward(s)
     for half in range(2):
-        acc = part_out[z, half]
+        acc = part_out[half, ahead[half]]
         for t in range(4):
-            if streams[t][0] == half:
-                rs_copy(t, hops[t] - 1).wait_recv()
-                acc = acc + arrived[t, hops[t] - 1].astype(F32)
+            if streams[t][0] == half and rs_hops[t]:
+                rs_copy(t, rs_hops[t] - 1).wait_recv()
+                acc = acc + arrived[t, rs_hops[t] - 1].astype(F32)
         mixed[half] = acc.astype(BF16)
     store(3, mixed, mixed_out).start()
 
     for t in range(4):
-        for s in range(hops[t]):
+        for s in range(ag_hops[t]):
             ag_copy(t, s).wait_send()
+        for s in range(rs_hops[t]):
             rs_copy(t, s).wait_send()
     linear.drain()
     trailing.drain()
+    w_drain()
+    for n in range(1, share):
+        attn_copy(n).wait_send()
+        g_copy(n).wait_send()
     for i, (src, dst) in enumerate(((gq, gq_out), (gk, gk_out), (gv, gv_out), (mixed, mixed_out))):
         store(i, src, dst).wait()
 
 
+def publish(*refs):
+    sem = refs[-1]
+    half = len(refs) // 2
+    copies = [pltpu.make_async_copy(refs[i], refs[half + i], sem.at[i]) for i in range(half)]
+    for copy in copies:
+        copy.start()
+    for copy in copies:
+        copy.wait()
+
+
 def on_device(sizes, length, query, key, value, block_mask, out_weight, cotangent):
-    nz, group, groups = sizes
+    nz, group, groups, share = sizes
     rows, width = query.shape
     heads = width // DH
     dim = out_weight.shape[1]
     sub = rows // nz // 2
+    span = nz // share
+    hop = max(span // 2, 1)
+    lines = group // 2
     cotangent = cotangent.reshape(2, sub, dim)
-    hop = nz // 2
+    out_weight = out_weight.reshape(2, lines, width // group, dim)
     piece = (heads * DH // group, DH)
     vmem, dma = pltpu.VMEM, pltpu.SemaphoreType.DMA
     any_space = pl.BlockSpec(memory_space=pl.ANY)
     square = (heads, rows, rows)
+    rows_of = (2, span, sub)
+    shapes = (
+        jax.ShapeDtypeStruct((2, sub, dim), BF16),
+        jax.ShapeDtypeStruct((rows, width), BF16),
+        jax.ShapeDtypeStruct((rows, width), BF16),
+        jax.ShapeDtypeStruct((rows, width), BF16),
+    )
     outs = pl.pallas_call(
         functools.partial(kernel, sizes, length),
-        out_shape=(
-            jax.ShapeDtypeStruct((2, sub, dim), BF16),
-            jax.ShapeDtypeStruct((rows, width), BF16),
-            jax.ShapeDtypeStruct((rows, width), BF16),
-            jax.ShapeDtypeStruct((rows, width), BF16),
-        ),
-        in_specs=[any_space, any_space, any_space, pl.BlockSpec(memory_space=pltpu.SMEM), any_space, any_space],
+        out_shape=shapes,
+        in_specs=[any_space] * 3 + [pl.BlockSpec(memory_space=pltpu.SMEM)] + [any_space] * 2,
         out_specs=(any_space,) * 4,
         scratch_shapes=[
             vmem((rows, width), BF16),
             vmem((rows, width), BF16),
             vmem((rows, width), BF16),
-            vmem((width, dim), BF16),
-            vmem((nz, 2, sub, dim), BF16),
+            vmem((share,) + out_weight.shape, BF16),
+            vmem(rows_of + (dim,), BF16),
             vmem(square, BF16),
             vmem(square, BF16),
             vmem((heads, rows, DH), F32),
             vmem((heads, rows, DH), F32),
-            vmem((rows, width), BF16),
-            vmem((nz, 2, sub, dim), F32),
+            vmem((nz, 2, sub, width), BF16),
+            vmem((share,) + rows_of + (width,), BF16),
+            vmem((share,) + rows_of + (width,), BF16),
+            vmem(rows_of + (dim,), F32),
+            vmem((share,) + rows_of + (width,), BF16),
+            vmem((share,) + rows_of + (width,), BF16),
+            vmem((nz, 2, sub, width), BF16),
             vmem((rows, width), BF16),
             vmem(square, BF16),
             vmem(square, BF16),
@@ -440,30 +670,40 @@
             vmem((2,) + piece, F32),
             vmem((2, groups) + piece, F32),
             vmem((2, group) + piece, F32),
-            dma((5,)),
+            dma((6,)),
             dma((4,)),
-            dma((4, hop)),
-            dma((4, hop)),
-            dma((4, hop)),
-            dma((4, hop)),
-            dma((2, group)),
-            dma((2, group)),
-            dma((2, groups)),
-            dma((2, groups)),
-            dma((2, group)),
-            dma((2, group)),
-        ],
+        ]
+        + [dma((4, hop))] * 4
+        + [dma((2, group))] * 2
+        + [dma((2, groups))] * 2
+        + [dma((2, group))] * 2
+        + [dma((2, share))] * 2
+        + [dma((groups,))] * 2
+        + [dma((4, lines // 2))] * 2
+        + [dma((4, lines // 2 + 1))] * 2
+        + [dma((lines,))] * 2
+        + [dma((2, groups // 2))] * 2
+        + [dma((2, groups // 2 + 1))] * 2
+        + [dma((share,))] * 4,
         compiler_params=pltpu.CompilerParams(
             collective_id=0, has_side_effects=True, vmem_limit_bytes=56 << 20
         ),
         name="mixer",
     )(query, key, value, block_mask, out_weight, cotangent)
+    outs = pl.pallas_call(
+        publish,
+        out_shape=shapes,
+        in_specs=[pl.BlockSpec(memory_space=pltpu.VMEM)] * 4,
+        out_specs=(any_space,) * 4,
+        scratch_shapes=[dma((4,))],
+        name="publish",
+    )(*outs)
     return (outs[0].reshape(2 * sub, dim),) + tuple(outs[1:])
 
 
 def solution(mesh):
     ctx = mesh.shape["ctx"]
-    sizes = (mesh.shape["head"], GROUP, ctx // GROUP)
+    sizes = (mesh.shape["head"], GROUP, ctx // GROUP, SHARE)
 
     def step(query, key, value, block_mask, out_weight, cotangent):
         return on_device(

time: 95.2 us -> 83.1 us (0.87)
  local copies, waits for them, and re-layouts: 6.52 us -> 0 us
  Pallas kernels: 87.7 us -> 82.3 us
    unnamed x4 -> x0, local copies, waits for them, and re-layouts: 6.52 us -> none
    pallas_call x1 -> x2, Pallas kernels: 87.7 us -> 82.3 us  [the longest x1 80.2 us: on_device(): pl.pallas_call(functools.partial(kernel, sizes, length), out_shape=shapes...]
where the time goes in v2:
time: 83.1 us; the launch traced here: 82.9 us
  Pallas kernels  82.3 us (99%)
    pallas_call x1, Pallas kernels, on_device(): pl.pallas_call(functools.partial(kernel, sizes, length), out_shape=shapes...  80.2 us
    pallas_call x1, Pallas kernels, on_device(): pl.pallas_call(publish, out_shape=shapes, in_specs=[pl.BlockSpec(memory_s...  2.13 us

profile of v2, /device:TPU:1, one launch (start us, length us, event | category | flops | bytes accessed | tf_op | source)
XLA Modules:
  0.0 82.9 jit_solution(6436727001201168818)
XLA Ops:
  0.6 80.2 %mixer.1 = (bf16[2,16,4096]{2,1,0:T(8,128)(2,1)}, bf16[384,256]{1,0:T(8,128)(2,1)}, bf16[384,256]{1,0:T(8,128)(2,1)}, bf16[384,256]{1,0:T(8,128)(2,1)}) custom-call(bf16[384,256]{1,0:T(8,128)(2,1)} %q_in.1, bf16[384,256]{1,0:T(8,128)(2,1)} %k_in.1, bf16[384,256]{1,0:T(8,128)(2,1)} %v_in.1, s32[3,3]{1,0:T(4,128)} %mask.1, bf16[2,8,16,4096]{3,2,1,0:T(8,128)(2,1)} %bitcast.3, ...), custom_call_target="tpu_custom_call" | custom-call | tf_op jit(solution)/shard_map/mixer/pallas_call | solution.py:634
  80.8 2.1 %publish.1 = (bf16[2,16,4096]{2,1,0:T(8,128)(2,1)}, bf16[384,256]{1,0:T(8,128)(2,1)}, bf16[384,256]{1,0:T(8,128)(2,1)}, bf16[384,256]{1,0:T(8,128)(2,1)}) custom-call(bf16[2,16,4096]{2,1,0:T(8,128)(2,1)} %get-tuple-element.12.refs_0_, bf16[384,256]{1,0:T(8,128)(2,1)} %get-tuple-element.13.refs_1_, bf16[384,256]{1,0:T(8,128)(2,1)} %get-tuple-element.14.refs_2_, ...), custom_call_target="tpu_custom_call" | custom-call | tf_op jit(solution)/shard_map/publish/pallas_call | solution.py:693

commit v3 on v2

--- a/solution.py
+++ b/solution.py
@@ -28,16 +28,11 @@
     return lax.dot_general(a, b, (((0,), (0,)), ((), ())), preferred_element_type=F32)
 
 
-def two(x):
-    high = x.astype(BF16)
-    return high, (x - high.astype(F32)).astype(BF16)
-
-
 class Scan:
-    def __init__(self, sizes, reverse, part, heard, sums, total, others, result, sems):
+    def __init__(self, sizes, reverse, part, heard, sums, back, total, others, result, sems):
         self.group, self.groups = sizes
         self.reverse = reverse
-        self.part, self.heard, self.sums = part, heard, sums
+        self.part, self.heard, self.sums, self.outgoing = part, heard, sums, back
         self.total, self.others, self.result = total, others, result
         self.send1, self.recv1, self.send2, self.recv2, self.send3, self.recv3 = sems
         ctx = lax.axis_index("ctx")
@@ -67,7 +62,7 @@
     def copy3(self, k):
         j = self.peer(k)
         return pltpu.make_async_remote_copy(
-            self.sums.at[j], self.result.at[self.r], self.send3.at[k], self.recv3.at[k],
+            self.outgoing.at[j], self.result.at[self.r], self.send3.at[k], self.recv3.at[k],
             device_id={"ctx": self.x * self.group + j}, device_id_type=MESH,
         )
 
@@ -100,9 +95,9 @@
             before = j > self.x if self.reverse else j < self.x
             base = base + jnp.where(before, self.others[j], 0.0)
         for p in range(self.group):
-            self.sums[p] = self.sums[p] + base
+            self.outgoing[p] = (self.sums[p] + base).astype(BF16)
         self.each(1, self.group, lambda k: self.copy3(k).start())
-        self.result[self.r] = self.sums[self.r]
+        self.result[self.r] = self.outgoing[self.r]
 
     def finish(self):
         self.each(1, self.group, lambda k: self.copy3(k).wait_recv())
@@ -120,7 +115,7 @@
     q, k, v, w, cot, probs, inner, soft, intra, attn, attn_sent, attn_held, part_out,
     g_sent, g_heard, g_rows, g, dsc, din,
     gk_part, gv_part, gq, gk, gv, mixed, first, arrived,
-    part, heard, sums, total, others, state,
+    part, heard, sums, back, total, others, state,
     load_sem, store_sem, ag_send, ag_recv, rs_send, rs_recv, s1, r1, s2, r2, s3, r3,
     wz_send, wz_recv, wx_send, wx_recv, wy_send, wy_recv, wc_send, wc_recv,
     vy_send, vy_recv, vx_send, vx_recv, vc_send, vc_recv,
@@ -177,6 +172,22 @@
     lax.fori_loop(1, groups, greet_far, 0)
     pl.semaphore_wait(barrier, 2 + share - 1 + group - 1 + groups - 1)
 
+    flying = {}
+
+    def go(make, *key):
+        make(*key).start()
+        flying[(make,) + key] = False
+
+    def got(make, *key):
+        make(*key).wait_recv()
+        flying[(make,) + key] = True
+
+    def land():
+        for (make, *key), heard_of in flying.items():
+            if not heard_of:
+                make(*key).wait_recv()
+            make(*key).wait_send()
+
     streams = ((0, 0), (0, 1), (1, 0), (1, 1))
     sign = (1, -1)
     ag_hops = [ahead[half ^ way] for half, way in streams]
@@ -198,9 +209,9 @@
     def ag_forward(s):
         for t in range(4):
             if 0 < s <= ag_hops[t]:
-                ag_copy(t, s - 1).wait_recv()
+                got(ag_copy, t, s - 1)
             if s < ag_hops[t]:
-                ag_copy(t, s).start()
+                go(ag_copy, t, s)
 
     def rs_copy(t, s):
         return pltpu.make_async_remote_copy(
@@ -218,15 +229,16 @@
                 if s == 0:
                     first[t] = own.astype(BF16)
                 else:
-                    rs_copy(t, s - 1).wait_recv()
+                    got(rs_copy, t, s - 1)
                     arrived[t, s - 1] = (arrived[t, s - 1].astype(F32) + own).astype(BF16)
-                rs_copy(t, s).start()
+                go(rs_copy, t, s)
 
     shared = pl.ds(1, share - 1)
-    wide = dim // 2
+    near = dim * 1 // 4
+    wide = dim - near
     few = lines // groups
-    left = pl.ds(pl.multiple_of(x * (wide // groups), wide // groups), wide // groups)
-    right = pl.ds(pl.multiple_of(wide + y * (wide // lines), wide // lines), wide // lines)
+    left = pl.ds(pl.multiple_of(x * (near // groups), near // groups), near // groups)
+    right = pl.ds(pl.multiple_of(near + y * (wide // lines), 128), wide // lines)
 
     def wz_copy(n, side):
         if side:
@@ -250,7 +262,7 @@
     def wy_piece(t, s):
         half, way = streams[t]
         from_y = lax.rem(y - sign[way] * s + lines, lines)
-        return w.at[shared, core, from_y, :, pl.ds(half * (wide // 2), wide // 2)]
+        return w.at[shared, core, from_y, :, pl.ds(half * (near // 2), near // 2)]
 
     def wy_copy(t, s):
         to = lax.rem(y + sign[streams[t][1]] + lines, lines)
@@ -278,7 +290,7 @@
     def vx_piece(way, s):
         from_x = lax.rem(x - sign[way] * s + groups, groups)
         halved = 2 * s == groups
-        columns = pl.ds(wide + way * (wide // 2), wide // 2) if halved else pl.ds(wide, wide)
+        columns = pl.ds(near + way * (wide // 2), wide // 2) if halved else pl.ds(near, wide)
         return w.at[shared, core, pl.ds(from_x * few, few), :, columns]
 
     vx_hops = groups // 2
@@ -286,7 +298,7 @@
     def vx_copy(way, s):
         from_x = lax.rem(x - sign[way] * s + groups, groups)
         halved = 2 * (s + 1) == groups
-        columns = pl.ds(wide + way * (wide // 2), wide // 2) if halved else pl.ds(wide, wide)
+        columns = pl.ds(near + way * (wide // 2), wide // 2) if halved else pl.ds(near, wide)
         piece = w.at[shared, core, pl.ds(from_x * few, few), :, columns]
         to = lax.rem(x + sign[way] + groups, groups)
         return pltpu.make_async_remote_copy(
@@ -303,66 +315,47 @@
     def w_start():
         for n in range(1, share):
             for side in range(2):
-                wz_copy(n, side).start()
+                go(wz_copy, n, side)
 
     def w_spread():
         for n in range(1, share):
-            wz_copy(n, 0).wait_recv()
+            got(wz_copy, n, 0)
         for n in range(1, groups):
-            wx_copy(n).start()
+            go(wx_copy, n)
         for n in range(1, share):
-            wz_copy(n, 1).wait_recv()
+            got(wz_copy, n, 1)
         for n in range(1, lines):
-            vy_copy(n).start()
+            go(vy_copy, n)
 
     def w_forward(s):
         if s == 0:
             for n in range(1, groups):
-                wx_copy(n).wait_recv()
+                got(wx_copy, n)
         for t in range(4):
             if 0 < s <= wy_hops[t]:
-                wy_copy(t, s - 1).wait_recv()
+                got(wy_copy, t, s - 1)
             if s < wy_hops[t]:
-                wy_copy(t, s).start()
+                go(wy_copy, t, s)
             if (t, s) in wc_all:
-                wc_copy(t, s).start()
+                go(wc_copy, t, s)
 
     def v_forward(s):
         if s == 0:
             for n in range(1, lines):
-                vy_copy(n).wait_recv()
+                got(vy_copy, n)
         for way in range(2):
             if 0 < s <= vx_hops:
-                vx_copy(way, s - 1).wait_recv()
+                got(vx_copy, way, s - 1)
             if s < vx_hops:
-                vx_copy(way, s).start()
+                go(vx_copy, way, s)
             if (way, s) in vc_all:
-                vc_copy(way, s).start()
+                go(vc_copy, way, s)
 
     def w_finish():
         for t, s in wc_all:
-            wc_copy(t, s).wait_recv()
+            got(wc_copy, t, s)
         for way, s in vc_all:
-            vc_copy(way, s).wait_recv()
-
-    def w_drain():
-        for n in range(1, share):
-            for side in range(2):
-                wz_copy(n, side).wait_send()
-        for n in range(1, groups):
-            wx_copy(n).wait_send()
-        for t in range(4):
-            for s in range(wy_hops[t]):
-                wy_copy(t, s).wait_send()
-        for t, s in wc_all:
-            wc_copy(t, s).wait_send()
-        for n in range(1, lines):
-            vy_copy(n).wait_send()
-        for way in range(2):
-            for s in range(vx_hops):
-                vx_copy(way, s).wait_send()
-        for way, s in vc_all:
-            vc_copy(way, s).wait_send()
+            got(vc_copy, way, s)
 
     def token(n, half, i):
         return along(n * span - ahead[half] + i)
@@ -378,7 +371,7 @@
             for half in range(2):
                 for i in range(span):
                     attn_sent[n, half, i] = attn[token(n, half, i), half]
-            attn_copy(n).start()
+            go(attn_copy, n)
         for half in range(2):
             for i in range(span):
                 attn_held[0, half, i] = attn[token(0, half, i), half]
@@ -396,11 +389,11 @@
             g_heard[0] = value
         else:
             g_sent[n] = value
-            g_copy(n).start()
+            go(g_copy, n)
 
     def g_collect():
         for n in range(1, share):
-            g_copy(n).wait_recv()
+            got(g_copy, n)
         for n in range(share):
             for half in range(2):
                 for i in range(span):
@@ -410,7 +403,7 @@
     def scan(which):
         return Scan(
             (group, groups), which == 1,
-            part.at[which], heard.at[which], sums.at[which], total.at[which],
+            part.at[which], heard.at[which], sums.at[which], back.at[which], total.at[which],
             others.at[which], state.at[which],
             [sem.at[which] for sem in (s1, r1, s2, r2, s3, r3)],
         )
@@ -453,8 +446,7 @@
             intra[h, here] = nn(a, v[upto, cols(h)])
 
     def attn_part(h):
-        high, low = two(get_state(0, h))
-        inter = nn(q[:, cols(h)], high) + nn(q[:, cols(h)], low)
+        inter = nn(q[:, cols(h)], get_state(0, h))
         value = (soft[h] + scale * (intra[h] + inter)).astype(BF16)
         attn[:, :, :, cols(h)] = value.reshape(nz, 2, -1, DH)
 
@@ -475,7 +467,7 @@
         lax.fori_loop(0, tiles, one, 0)
 
     def backward_rows(h):
-        high, low = two(get_state(0, h))
+        earlier = get_state(0, h)
         for i in range(blocks):
             here, upto = slice(i * blk, (i + 1) * blk), slice(0, (i + 1) * blk)
             gi = g[here, cols(h)]
@@ -487,7 +479,7 @@
             din[h, here, upto] = di
             kk = k[upto, cols(h)]
             gq[here, cols(h)] = (
-                nn(ds, kk) + scale * (nn(di, kk) + (nt(gi, high) + nt(gi, low)))
+                nn(ds, kk) + scale * (nn(di, kk) + nt(gi, earlier))
             ).astype(BF16)
 
     def backward_columns(h):
@@ -502,20 +494,37 @@
             )
 
     def backward_last(h):
-        high, low = two(get_state(1, h))
+        later = get_state(1, h)
         vv, kk = v[:, cols(h)], k[:, cols(h)]
-        gk[:, cols(h)] = (gk_part[:, cols(h)] + (nt(vv, high) + nt(vv, low))).astype(BF16)
-        gv[:, cols(h)] = (gv_part[:, cols(h)] + (nn(kk, high) + nn(kk, low))).astype(BF16)
+        gk[:, cols(h)] = (gk_part[:, cols(h)] + nt(vv, later)).astype(BF16)
+        gv[:, cols(h)] = (gv_part[:, cols(h)] + nn(kk, later)).astype(BF16)
 
     def store(i, src, dst):
         return pltpu.make_async_copy(src, dst, store_sem.at[i])
 
+    def own_state():
+        loads[0].wait()
+        loads[1].wait()
+        for h in range(heads):
+            put_part(0, h, tn(k[:, cols(h)], v[:, cols(h)]))
+
+    def own_grad():
+        for h in range(heads):
+            put_part(1, h, scale * tn(q[:, cols(h)], g[:, cols(h)]))
+
+    def finish_sum():
+        for half in range(2):
+            acc = part_out[half, ahead[half]]
+            for t in range(4):
+                if streams[t][0] == half and rs_hops[t]:
+                    got(rs_copy, t, rs_hops[t] - 1)
+                    acc = acc + arrived[t, rs_hops[t] - 1].astype(F32)
+            mixed[half] = acc.astype(BF16)
+
+    results = ((gq, gq_out), (gk, gk_out), (gv, gv_out), (mixed, mixed_out))
     w_start()
     ag_forward(0)
-    loads[0].wait()
-    loads[1].wait()
-    for h in range(heads):
-        put_part(0, h, tn(k[:, cols(h)], v[:, cols(h)]))
+    own_state()
     linear.start()
     loads[2].wait()
     w_spread()
@@ -524,8 +533,7 @@
     linear.middle()
     w_forward(0)
     v_forward(0)
-    for h in range(1, heads):
-        softmax_part(h)
+    softmax_part(1)
     w_forward(1)
     linear.back()
     ag_forward(2)
@@ -538,64 +546,38 @@
         attn_part(h)
     attn_exchange()
     v_forward(2)
-    for s in range(4, max(wy_hops) + 1):
-        w_forward(s)
-    for s in range(4, max(ag_hops) + 1):
-        ag_forward(s)
-    w_finish()
-
     for load in loads[3:]:
         load.wait()
-    for n in reversed(range(share)):
-        grad_attn_part(n)
-    for n in range(1, share):
-        attn_copy(n).wait_recv()
+    grad_attn_part(0)
+    w_forward(4)
+    w_finish()
+    grad_attn_part(1)
+    got(attn_copy, 1)
     project()
     rs_forward(0)
     g_collect()
-    for h in range(heads):
-        put_part(1, h, scale * tn(q[:, cols(h)], g[:, cols(h)]))
+    own_grad()
     trailing.start()
     backward_rows(0)
+    backward_rows(1)
+    store(0, gq, gq_out).start()
     rs_forward(1)
-    for h in range(1, heads):
-        backward_rows(h)
-    store(0, gq, gq_out).start()
     trailing.middle()
+    backward_columns(0)
+    backward_columns(1)
+    trailing.back()
     rs_forward(2)
-    backward_columns(0)
-    trailing.back()
-    rs_forward(3)
-    for h in range(1, heads):
-        backward_columns(h)
     trailing.finish()
     for h in range(heads):
         backward_last(h)
     store(1, gk, gk_out).start()
     store(2, gv, gv_out).start()
-    for s in range(4, max(rs_hops)):
-        rs_forward(s)
-    for half in range(2):
-        acc = part_out[half, ahead[half]]
-        for t in range(4):
-            if streams[t][0] == half and rs_hops[t]:
-                rs_copy(t, rs_hops[t] - 1).wait_recv()
-                acc = acc + arrived[t, rs_hops[t] - 1].astype(F32)
-        mixed[half] = acc.astype(BF16)
+    finish_sum()
     store(3, mixed, mixed_out).start()
-
-    for t in range(4):
-        for s in range(ag_hops[t]):
-            ag_copy(t, s).wait_send()
-        for s in range(rs_hops[t]):
-            rs_copy(t, s).wait_send()
+    land()
     linear.drain()
     trailing.drain()
-    w_drain()
-    for n in range(1, share):
-        attn_copy(n).wait_send()
-        g_copy(n).wait_send()
-    for i, (src, dst) in enumerate(((gq, gq_out), (gk, gk_out), (gv, gv_out), (mixed, mixed_out))):
+    for i, (src, dst) in enumerate(results):
         store(i, src, dst).wait()
 
 
@@ -667,9 +649,10 @@
             vmem((2, group) + piece, F32),
             vmem((2, group) + piece, F32),
             vmem((2, group) + piece, F32),
+            vmem((2, group) + piece, BF16),
             vmem((2,) + piece, F32),
             vmem((2, groups) + piece, F32),
-            vmem((2, group) + piece, F32),
+            vmem((2, group) + piece, BF16),
             dma((6,)),
             dma((4,)),
         ]

time: 83.1 us -> 80.5 us (0.969)
  Pallas kernels: 82.3 us -> 79.5 us
    pallas_call x1, Pallas kernels: 80.2 us -> 77.4 us  [on_device(): pl.pallas_call(functools.partial(kernel, sizes, length), out_shape=shapes...]
where the time goes in v3:
time: 80.5 us; the launch traced here: 80.2 us
  Pallas kernels  79.5 us (99%)
    pallas_call x1, Pallas kernels, on_device(): pl.pallas_call(functools.partial(kernel, sizes, length), out_shape=shapes...  77.4 us
    pallas_call x1, Pallas kernels, on_device(): pl.pallas_call(publish, out_shape=shapes, in_specs=[pl.BlockSpec(memory_s...  2.13 us

profile of v3, /device:TPU:1, one launch (start us, length us, event | category | flops | bytes accessed | tf_op | source)
XLA Modules:
  0.0 80.2 jit_solution(2377064585702903748)
XLA Ops:
  0.6 77.4 %mixer.1 = (bf16[2,16,4096]{2,1,0:T(8,128)(2,1)}, bf16[384,256]{1,0:T(8,128)(2,1)}, bf16[384,256]{1,0:T(8,128)(2,1)}, bf16[384,256]{1,0:T(8,128)(2,1)}) custom-call(bf16[384,256]{1,0:T(8,128)(2,1)} %q_in.1, bf16[384,256]{1,0:T(8,128)(2,1)} %k_in.1, bf16[384,256]{1,0:T(8,128)(2,1)} %v_in.1, s32[3,3]{1,0:T(4,128)} %mask.1, bf16[2,8,16,4096]{3,2,1,0:T(8,128)(2,1)} %bitcast.3, ...), custom_call_target="tpu_custom_call" | custom-call | tf_op jit(solution)/shard_map/mixer/pallas_call | solution.py:616
  78.0 2.1 %publish.1 = (bf16[2,16,4096]{2,1,0:T(8,128)(2,1)}, bf16[384,256]{1,0:T(8,128)(2,1)}, bf16[384,256]{1,0:T(8,128)(2,1)}, bf16[384,256]{1,0:T(8,128)(2,1)}) custom-call(bf16[2,16,4096]{2,1,0:T(8,128)(2,1)} %get-tuple-element.12.refs_0_, bf16[384,256]{1,0:T(8,128)(2,1)} %get-tuple-element.13.refs_1_, bf16[384,256]{1,0:T(8,128)(2,1)} %get-tuple-element.14.refs_2_, ...), custom_call_target="tpu_custom_call" | custom-call | tf_op jit(solution)/shard_map/publish/pallas_call | solution.py:676

commit v4 on v3

--- a/solution.py
+++ b/solution.py
@@ -117,7 +117,7 @@
     gk_part, gv_part, gq, gk, gv, mixed, first, arrived,
     part, heard, sums, back, total, others, state,
     load_sem, store_sem, ag_send, ag_recv, rs_send, rs_recv, s1, r1, s2, r2, s3, r3,
-    wz_send, wz_recv, wx_send, wx_recv, wy_send, wy_recv, wc_send, wc_recv,
+    wz_send, wz_recv,
     vy_send, vy_recv, vx_send, vx_recv, vc_send, vc_recv,
     at_send, at_recv, gt_send, gt_recv,
 ):
@@ -234,41 +234,14 @@
                 go(rs_copy, t, s)
 
     shared = pl.ds(1, share - 1)
-    near = dim * 1 // 4
-    wide = dim - near
     few = lines // groups
-    left = pl.ds(pl.multiple_of(x * (near // groups), near // groups), near // groups)
-    right = pl.ds(pl.multiple_of(near + y * (wide // lines), 128), wide // lines)
-
-    def wz_copy(n, side):
-        if side:
-            at = (core, pl.ds(x * few, few), slice(None), right)
-        else:
-            at = (core, y, slice(None), left)
-        return pltpu.make_async_remote_copy(
-            w_in.at[at], w.at[(share - n,) + at], wz_send.at[side, n], wz_recv.at[side, n],
+    right = pl.ds(pl.multiple_of(y * (dim // lines), dim // lines), dim // lines)
+
+    def wz_copy(n):
+        at = (core, pl.ds(x * few, few), slice(None), right)
+        return pltpu.make_async_remote_copy(
+            w_in.at[at], w.at[(share - n,) + at], wz_send.at[n], wz_recv.at[n],
             device_id={"head": along(n * span)}, device_id_type=MESH,
-        )
-
-    def wx_copy(n):
-        piece = w.at[shared, core, y, :, left]
-        return pltpu.make_async_remote_copy(
-            piece, piece, wx_send.at[n], wx_recv.at[n],
-            device_id={"ctx": lax.rem(x + n, groups) * group + r}, device_id_type=MESH,
-        )
-
-    wy_hops = [lines // 2 if half == way else lines - 1 - lines // 2 for half, way in streams]
-
-    def wy_piece(t, s):
-        half, way = streams[t]
-        from_y = lax.rem(y - sign[way] * s + lines, lines)
-        return w.at[shared, core, from_y, :, pl.ds(half * (near // 2), near // 2)]
-
-    def wy_copy(t, s):
-        to = lax.rem(y + sign[streams[t][1]] + lines, lines)
-        return pltpu.make_async_remote_copy(
-            wy_piece(t, s), wy_piece(t, s), wy_send.at[t, s], wy_recv.at[t, s],
-            device_id={"ctx": x * group + to * 2 + core}, device_id_type=MESH,
         )
 
     def to_core(piece, send, recv):
@@ -276,9 +249,6 @@
             piece, piece, send, recv,
             device_id={"ctx": x * group + y * 2 + 1 - core}, device_id_type=MESH,
         )
-
-    def wc_copy(t, s):
-        return to_core(wy_piece(t, s), wc_send.at[t, s], wc_recv.at[t, s])
 
     def vy_copy(n):
         piece = w.at[shared, core, pl.ds(x * few, few), :, right]
@@ -290,7 +260,7 @@
     def vx_piece(way, s):
         from_x = lax.rem(x - sign[way] * s + groups, groups)
         halved = 2 * s == groups
-        columns = pl.ds(near + way * (wide // 2), wide // 2) if halved else pl.ds(near, wide)
+        columns = pl.ds(way * (dim // 2), dim // 2) if halved else pl.ds(0, dim)
         return w.at[shared, core, pl.ds(from_x * few, few), :, columns]
 
     vx_hops = groups // 2
@@ -298,7 +268,7 @@
     def vx_copy(way, s):
         from_x = lax.rem(x - sign[way] * s + groups, groups)
         halved = 2 * (s + 1) == groups
-        columns = pl.ds(near + way * (wide // 2), wide // 2) if halved else pl.ds(near, wide)
+        columns = pl.ds(way * (dim // 2), dim // 2) if halved else pl.ds(0, dim)
         piece = w.at[shared, core, pl.ds(from_x * few, few), :, columns]
         to = lax.rem(x + sign[way] + groups, groups)
         return pltpu.make_async_remote_copy(
@@ -309,35 +279,17 @@
     def vc_copy(way, s):
         return to_core(vx_piece(way, s), vc_send.at[way, s], vc_recv.at[way, s])
 
-    wc_all = [(0, 0), (2, 0)] + [(t, s + 1) for t in range(4) for s in range(wy_hops[t])]
     vc_all = [(0, 0)] + [(way, s + 1) for way in range(2) for s in range(vx_hops)]
 
     def w_start():
         for n in range(1, share):
-            for side in range(2):
-                go(wz_copy, n, side)
+            go(wz_copy, n)
 
     def w_spread():
         for n in range(1, share):
-            got(wz_copy, n, 0)
-        for n in range(1, groups):
-            go(wx_copy, n)
-        for n in range(1, share):
-            got(wz_copy, n, 1)
+            got(wz_copy, n)
         for n in range(1, lines):
             go(vy_copy, n)
-
-    def w_forward(s):
-        if s == 0:
-            for n in range(1, groups):
-                got(wx_copy, n)
-        for t in range(4):
-            if 0 < s <= wy_hops[t]:
-                got(wy_copy, t, s - 1)
-            if s < wy_hops[t]:
-                go(wy_copy, t, s)
-            if (t, s) in wc_all:
-                go(wc_copy, t, s)
 
     def v_forward(s):
         if s == 0:
@@ -352,8 +304,6 @@
                 go(vc_copy, way, s)
 
     def w_finish():
-        for t, s in wc_all:
-            got(wc_copy, t, s)
         for way, s in vc_all:
             got(vc_copy, way, s)
 
@@ -531,15 +481,11 @@
     softmax_part(0)
     ag_forward(1)
     linear.middle()
-    w_forward(0)
     v_forward(0)
     softmax_part(1)
-    w_forward(1)
     linear.back()
     ag_forward(2)
-    w_forward(2)
     v_forward(1)
-    w_forward(3)
     ag_forward(3)
     linear.finish()
     for h in range(heads):
@@ -549,7 +495,6 @@
     for load in loads[3:]:
         load.wait()
     grad_attn_part(0)
-    w_forward(4)
     w_finish()
     grad_attn_part(1)
     got(attn_copy, 1)
@@ -660,10 +605,7 @@
         + [dma((2, group))] * 2
         + [dma((2, groups))] * 2
         + [dma((2, group))] * 2
-        + [dma((2, share))] * 2
-        + [dma((groups,))] * 2
-        + [dma((4, lines // 2))] * 2
-        + [dma((4, lines // 2 + 1))] * 2
+        + [dma((share,))] * 2
         + [dma((lines,))] * 2
         + [dma((2, groups // 2))] * 2
         + [dma((2, groups // 2 + 1))] * 2

time: 80.5 us -> 79.6 us (0.989)
  no operation moved by 1% of the time
where the time goes in v4:
time: 79.6 us; the launch traced here: 79.4 us
  Pallas kernels  78.8 us (99%)
    pallas_call x1, Pallas kernels, on_device(): pl.pallas_call(functools.partial(kernel, sizes, length), out_shape=shapes...  76.6 us
    pallas_call x1, Pallas kernels, on_device(): pl.pallas_call(publish, out_shape=shapes, in_specs=[pl.BlockSpec(memory_s...  2.13 us

profile of v4, /device:TPU:1, one launch (start us, length us, event | category | flops | bytes accessed | tf_op | source)
XLA Modules:
  0.0 79.4 jit_solution(499463581031685123)
XLA Ops:
  0.6 76.6 %mixer.1 = (bf16[2,16,4096]{2,1,0:T(8,128)(2,1)}, bf16[384,256]{1,0:T(8,128)(2,1)}, bf16[384,256]{1,0:T(8,128)(2,1)}, bf16[384,256]{1,0:T(8,128)(2,1)}) custom-call(bf16[384,256]{1,0:T(8,128)(2,1)} %q_in.1, bf16[384,256]{1,0:T(8,128)(2,1)} %k_in.1, bf16[384,256]{1,0:T(8,128)(2,1)} %v_in.1, s32[3,3]{1,0:T(4,128)} %mask.1, bf16[2,8,16,4096]{3,2,1,0:T(8,128)(2,1)} %bitcast.3, ...), custom_call_target="tpu_custom_call" | custom-call | tf_op jit(solution)/shard_map/mixer/pallas_call | solution.py:561
  77.3 2.1 %publish.1 = (bf16[2,16,4096]{2,1,0:T(8,128)(2,1)}, bf16[384,256]{1,0:T(8,128)(2,1)}, bf16[384,256]{1,0:T(8,128)(2,1)}, bf16[384,256]{1,0:T(8,128)(2,1)}) custom-call(bf16[2,16,4096]{2,1,0:T(8,128)(2,1)} %get-tuple-element.12.refs_0_, bf16[384,256]{1,0:T(8,128)(2,1)} %get-tuple-element.13.refs_1_, bf16[384,256]{1,0:T(8,128)(2,1)} %get-tuple-element.14.refs_2_, ...), custom_call_target="tpu_custom_call" | custom-call | tf_op jit(solution)/shard_map/publish/pallas_call | solution.py:618
